TPU v7x, 32 devices: a whole 2x2x4 slice. The times are simulated.
32 devices in a mesh: dom: 8 (over z, y), rows: 4 (over x, core).
Axes of the slice: x: 2, y: 2, z: 4, core: 2. Of those that a mesh axis runs over, the one named last changes fastest.
Arguments:
- fields: float32 [8, 3, 128, 4096], P('dom', None, 'rows'), may hold values from -6 to 6
- depth: float32 [128, 4096], P('rows'), may hold values from 1.5 to 6
- obs_index: int32 [256], replicated, may hold values from 0 to 524287, as said below
- obs_value: float32 [256], replicated, may hold values from -6 to 6
- obs_var: float32 [256], replicated, may hold values from 0.5 to 5
- parent_lookup: int32 [8], replicated, may hold values from 0 to 7, as said below
Outputs:
- log_weights: float32 [8], P('dom')
- posterior_members: float32 [8, 3, 128, 4096], P('dom', None, 'rows')
Inputs may be any that keep to these rules, and one draw needn't show every extreme that they name: `parent_lookup`: every value is the index of a particle; 0 and 7 each appear; values may repeat. `obs_index`: indices of grid cells, possibly repeated; the first and last cell each appear.
All inputs are finite; a program needn't handle non-finite values.
Results may differ from a plain program's by a relative error of at most 0.00003.
Values sent between devices are 32-bit elements; how exact they have to be, the bound alone decides.
No kernel may reach another device: no remote copies, remote signals or barrier semaphores. Data moves between devices by JAX's collectives and lax.ppermute only.
A program may use at most 64 MiB of HBM per device.

v0:
```python
import jax
import jax.numpy as jnp
from jax import lax
from jax.experimental import pallas as pl
from jax.experimental.pallas import tpu as pltpu
from jax.sharding import PartitionSpec as P

STEPS = 4
HALO = 2 * STEPS
LANES = 128
VMEM_BYTES = 48 * 2**20

time_step = 0.5
coriolis = 0.2

in_vmem = pl.BlockSpec(memory_space=pltpu.VMEM)
in_smem = pl.BlockSpec(memory_space=pltpu.SMEM)
in_hbm = pl.BlockSpec(memory_space=pltpu.HBM)


def model_steps(h_ref, u_ref, v_ref, d_ref, top_open=None, bottom_open=None):
    n_rows, n_cols = h_ref.shape
    h_ref[...] = h_ref[...] * (0.5 * time_step)
    d_ref[...] = d_ref[...] * (0.25 * time_step * time_step)

    def cols(a):
        return pltpu.roll(a, n_cols - 1, 1) - pltpu.roll(a, 1, 1)

    def rows(a):
        return pltpu.roll(a, n_rows - 1, 0) - pltpu.roll(a, 1, 0)

    def step(_, carry):
        u = u_ref[...]
        v = v_ref[...]
        d = d_ref[...]
        h = h_ref[...] - (cols(d * u) + rows(d * v))
        if top_open is not None:
            h = jnp.concatenate(
                [h[:HALO] * top_open, h[HALO : n_rows - HALO], h[n_rows - HALO :] * bottom_open], axis=0
            )
        h_ref[...] = h
        u = u - cols(h) + (time_step * coriolis) * v
        u_ref[...] = u
        v_ref[...] = v - rows(h) - (time_step * coriolis) * u
        return carry

    lax.fori_loop(0, STEPS, step, 0)
    h_ref[...] = h_ref[...] * (2.0 / time_step)


def store_pieces(at_ref, outs, state, rows_of):
    width = outs[0].shape[-1]
    for m, out in enumerate(outs):
        start = pl.multiple_of(jnp.bitwise_xor(at_ref[0], m) * width, LANES)
        for k, ref in enumerate(state[:3]):
            out[k] = rows_of(ref, pl.ds(start, width))


def inner_kernel(at_ref, fields_ref, depth_ref, *refs):
    outs, (h_ref, head_ref, tail_ref), state = refs[:-7], refs[-7:-4], refs[-4:]
    n_rows = depth_ref.shape[0]
    for k in range(4):
        field = depth_ref[...] if k == 3 else fields_ref[0, k]
        state[k][...] = field
        head_ref[k] = field[:HALO]
        tail_ref[k] = field[n_rows - HALO :]
    model_steps(*state)
    h_ref[...] = state[0][HALO : n_rows - HALO]
    store_pieces(at_ref, outs, state, lambda ref, at: ref[HALO : n_rows - HALO, at])


def outer_kernel(at_ref, fields_ref, depth_ref, above_ref, below_ref, *refs):
    outs, h_ref, state = refs[:-5], refs[-5], refs[-4:]
    n_rows = depth_ref.shape[0]
    for k in range(4):
        state[k][:HALO] = above_ref[k]
        state[k][HALO : HALO + n_rows] = depth_ref[...] if k == 3 else fields_ref[0, k]
        state[k][HALO + n_rows :] = below_ref[k]
    model_steps(*state, at_ref[1].astype(jnp.float32), at_ref[2].astype(jnp.float32))

    def outer_rows(ref, at):
        return jnp.concatenate([ref[HALO : 2 * HALO, at], ref[n_rows : n_rows + HALO, at]], axis=0)

    h_ref[...] = outer_rows(state[0], pl.ds(0, depth_ref.shape[1]))
    store_pieces(at_ref, outs, state, outer_rows)


def forecast(kernel, name, at, arrays, n_rows, n_cols, count, window_rows, extra=()):
    shapes = [(3, n_rows, n_cols // count)] * count + [(n_rows, n_cols)] + list(extra)
    outs = pl.pallas_call(
        kernel,
        out_shape=[jax.ShapeDtypeStruct(shape, jnp.float32) for shape in shapes],
        in_specs=[in_smem] + [in_vmem] * len(arrays),
        out_specs=[in_vmem] * len(shapes),
        scratch_shapes=[pltpu.VMEM((window_rows, n_cols), jnp.float32)] * 4,
        compiler_params=pltpu.CompilerParams(vmem_limit_bytes=VMEM_BYTES),
        name=name,
    )(at, *arrays)
    return list(outs[:count]), outs[count:]


def misfit_kernel(at_ref, index_ref, value_ref, var_ref, inner_ref, outer_ref, out_ref, total_ref):
    inner_rows, n_cols = inner_ref.shape
    n_rows = inner_rows + 2 * HALO
    base = at_ref[3] * (n_rows * n_cols)
    row_in = lax.broadcasted_iota(jnp.int32, (8, LANES), 0)
    lane_in = lax.broadcasted_iota(jnp.int32, (8, LANES), 1)

    def tile(ref, row, col):
        first_row = pl.multiple_of(jnp.bitwise_and(row, -8), 8)
        first_col = pl.multiple_of(jnp.bitwise_and(col, -LANES), LANES)
        return ref[pl.ds(first_row, 8), pl.ds(first_col, LANES)]

    def point(k, carry):
        offset = index_ref[k] - base

        @pl.when(jnp.logical_and(offset >= 0, offset < n_rows * n_cols))
        def _():
            row = lax.div(offset, n_cols)
            col = offset - row * n_cols
            inner_row = row - HALO
            is_inner = jnp.logical_and(inner_row >= 0, inner_row < inner_rows)
            outer_row = jnp.where(row < HALO, row, row - inner_rows)
            hit = (row_in == jnp.bitwise_and(row, 7)) & (lane_in == jnp.bitwise_and(col, LANES - 1))

            def add(seen):
                total_ref[...] += jnp.where(hit, (value_ref[k] - seen) ** 2 / var_ref[k], 0.0)

            @pl.when(is_inner)
            def _():
                add(tile(inner_ref, inner_row, col))

            @pl.when(jnp.logical_not(is_inner))
            def _():
                add(tile(outer_ref, outer_row, col))

        return carry

    total_ref[...] = jnp.zeros_like(total_ref)
    lax.fori_loop(0, index_ref.shape[0], point, 0, unroll=8)
    out_ref[...] = jnp.broadcast_to(jnp.sum(total_ref[...]), out_ref.shape)


def misfit(at, obs_index, obs_value, obs_var, inner, outer):
    return pl.pallas_call(
        misfit_kernel,
        out_shape=jax.ShapeDtypeStruct((8, LANES), jnp.float32),
        in_specs=[in_smem] * 4 + [in_vmem] * 2,
        out_specs=in_vmem,
        scratch_shapes=[pltpu.VMEM((8, LANES), jnp.float32)],
        compiler_params=pltpu.CompilerParams(vmem_limit_bytes=VMEM_BYTES),
        name="misfit",
    )(at, obs_index, obs_value, obs_var, inner, outer)[0, 0]


def sum_over(x, axis):
    count = lax.axis_size(axis)
    step = 1
    while step < count:
        x = x + lax.ppermute(x, axis, [(i, i ^ step) for i in range(count)])
        step *= 2
    return x


def log_weight(loglik):
    slots = lax.broadcasted_iota(jnp.int32, (lax.axis_size("dom"),), 0)
    every = sum_over(jnp.where(slots == lax.axis_index("dom"), loglik, 0.0), "dom")
    peak = jnp.max(every)
    total = jnp.sum(jnp.exp(every - peak))
    return (loglik - (peak + jnp.log(total)))[None]


def place(at, pieces, spans, shape, into=None):
    count = len(pieces)
    n_cols = shape[-1]
    width = n_cols // count

    def kernel(at_ref, *refs):
        srcs = refs[:count]
        dst, sems = refs[-2], refs[-1]
        copies = []
        for m in range(count):
            first = pl.multiple_of(jnp.bitwise_xor(at_ref[0], m) * width, LANES)
            for s, (src_row, dst_row, size) in enumerate(spans):
                copies.append(
                    pltpu.make_async_copy(
                        srcs[m].at[:, pl.ds(src_row, size), :],
                        dst.at[0, :, pl.ds(dst_row, size), pl.ds(first, width)],
                        sems.at[m * len(spans) + s],
                    )
                )
        for c in copies:
            c.start()
        for c in copies:
            c.wait()

    extra = [] if into is None else [into]
    return pl.pallas_call(
        kernel,
        out_shape=pltpu.HBM(shape, jnp.float32),
        in_specs=[in_smem] + [in_vmem] * count + [in_hbm] * len(extra),
        out_specs=in_hbm,
        scratch_shapes=[pltpu.SemaphoreType.DMA((count * len(spans),))],
        input_output_aliases={} if into is None else {count + 1: 0},
        compiler_params=pltpu.CompilerParams(vmem_limit_bytes=VMEM_BYTES),
        name="place",
    )(at, *pieces, *extra)


def route_kernel(at_ref, parents_ref, out_ref, *, half):
    own = at_ref[0]
    side = at_ref[4]
    parents = [parents_ref[s] for s in range(2 * half)]

    def ranks(first):
        other = half - first
        running = jnp.int32(0)
        needed, rank = [], []
        for q in range(half):
            hit = jnp.int32(0)
            for s in range(half):
                hit = hit | jnp.where(parents[other + s] == first + q, 1, 0).astype(jnp.int32)
            needed.append(hit)
            rank.append(running)
            running = running + hit
        return needed, rank, running

    low = ranks(0)
    high = ranks(half)
    out_ref[0] = jnp.maximum(low[2], high[2])
    mine = [jnp.where(side == 0, a, b) for a, b in zip(low[0], high[0])]
    my_rank = [jnp.where(side == 0, a, b) for a, b in zip(low[1], high[1])]
    other_rank = [jnp.where(side == 0, b, a) for a, b in zip(low[1], high[1])]
    for k in range(half):
        chosen = jnp.int32(0)
        for q in range(half):
            chosen = jnp.where((mine[q] == 1) & (my_rank[q] == k), q, chosen)
        out_ref[1 + k] = jnp.bitwise_xor(chosen, own)
    for m in range(half):
        slot = jnp.bitwise_xor(own, m)
        parent = jnp.int32(0)
        for s in range(half):
            parent = jnp.where(slot == s, jnp.where(side == 0, parents[s], parents[half + s]), parent)
        local = parent - side * half
        remote = parent - (1 - side) * half
        from_rank = jnp.int32(0)
        for q in range(half):
            from_rank = jnp.where(remote == q, other_rank[q], from_rank)
        is_local = jnp.logical_and(local >= 0, local < half)
        out_ref[1 + half + m] = jnp.where(is_local, jnp.bitwise_xor(local, own), half + from_rank)


def route(at, parent_lookup, half):
    return pl.pallas_call(
        lambda *refs: route_kernel(*refs, half=half),
        out_shape=jax.ShapeDtypeStruct((1 + 2 * half,), jnp.int32),
        in_specs=[in_smem, in_smem],
        out_specs=in_smem,
        name="route",
    )(at, parent_lookup)


def to_mate(x, m):
    return lax.ppermute(x, "dom", [(i, i ^ m) for i in range(lax.axis_size("dom"))])


def among_mates(pieces):
    return [x if m == 0 else to_mate(x, m) for m, x in enumerate(pieces)]


def pick(routes, first, count, sources, stacks=(), stacked=False):
    block = sources[0].shape

    def kernel(routes_ref, *refs):
        n_in = len(sources) + len(stacks)
        srcs = [(ref, None) for ref in refs[: len(sources)]]
        srcs += [(ref, k) for ref in refs[len(sources) : n_in] for k in range(ref.shape[0])]
        for m in range(count):
            which = routes_ref[first + m]
            for s, (src, k) in enumerate(srcs):

                @pl.when(which == s)
                def _(m=m, src=src, k=k):
                    value = src[...] if k is None else src[k]
                    if stacked:
                        refs[n_in][m] = value
                    else:
                        refs[n_in + m][...] = value

    shapes = [(count,) + block] if stacked else [block] * count
    return pl.pallas_call(
        kernel,
        out_shape=[jax.ShapeDtypeStruct(shape, jnp.float32) for shape in shapes],
        in_specs=[in_smem] + [in_vmem] * (len(sources) + len(stacks)),
        out_specs=[in_vmem] * len(shapes),
        compiler_params=pltpu.CompilerParams(vmem_limit_bytes=VMEM_BYTES),
        name="pick",
    )(routes, *sources, *stacks)


def chosen(held, routes, crossing):
    return pick(routes, 1, crossing, held, stacked=True)[0]


def for_slots(held, got, routes):
    return pick(routes, 1 + len(held), len(held), held, [got])


def after(x, *earlier):
    return lax.optimization_barrier((x, earlier))[0]


def halo_rows(head, tail):
    count = lax.axis_size("rows")
    above = lax.ppermute(tail, "rows", [(i, i + 1) for i in range(count - 1)])
    below = lax.ppermute(head, "rows", [(i + 1, i) for i in range(count - 1)])
    return above, below


def inner_forecast(at, fields, depth, count):
    n_rows, n_cols = depth.shape
    rim = (4, HALO, n_cols)
    return forecast(inner_kernel, "inner", at, (fields, depth), n_rows - 2 * HALO, n_cols, count, n_rows, (rim, rim))


def outer_forecast(at, fields, depth, above, below, count):
    n_rows, n_cols = depth.shape
    arrays = (fields, depth, above, below)
    return forecast(outer_kernel, "outer", at, arrays, 2 * HALO, n_cols, count, n_rows + 2 * HALO)


def cycle(crossing, routes, at, fields, depth, obs_index, obs_value, obs_var):
    half = lax.axis_size("dom") // 2
    n_rows, n_cols = depth.shape
    inner, (inner_h, head, tail) = inner_forecast(at, fields, depth, half)
    above, below = halo_rows(head, tail)
    inner_held = among_mates(inner)
    outer, (outer_h,) = outer_forecast(at, fields, depth, above, below, half)
    outer_held = among_mates(outer)
    inner_chosen = chosen(after(inner_held, outer), routes, crossing)
    inner_got = to_mate(inner_chosen, half)
    misfit_sum = misfit(at, obs_index, obs_value, obs_var, inner_h, after(outer_h, inner_chosen))
    loglik = sum_over(-0.5 * misfit_sum, "rows")
    outer_chosen = chosen(after(outer_held, loglik), routes, crossing)
    outer_got = to_mate(outer_chosen, half)
    inner_done = among_mates(for_slots(inner_held, after(inner_got, outer_chosen), routes))
    log_weights = log_weight(after(loglik, outer_chosen))
    outer_slots = for_slots(outer_held, outer_got, routes)
    outer_done = among_mates(outer_slots)
    members = place(at, after(inner_done, outer_slots), ((0, HALO, n_rows - 2 * HALO),), fields.shape)
    members = place(at, outer_done, ((0, 0, HALO), (HALO, n_rows - HALO, HALO)), fields.shape, members)
    return log_weights, members


def shards(fields, depth, obs_index, obs_value, obs_var, parent_lookup):
    rows_at = lax.axis_index("rows")
    dom_at = lax.axis_index("dom")
    half = lax.axis_size("dom") // 2
    at = jnp.stack(
        [dom_at % half, rows_at > 0, rows_at < lax.axis_size("rows") - 1, rows_at, dom_at // half]
    ).astype(jnp.int32)
    if half == 4:
        routes = route(at, parent_lookup, half)
        branches = [
            (lambda r, a, *rest, c=c: cycle(c, r, a, *rest)) for c in range(1, half + 1)
        ]
        return lax.switch(
            jnp.clip(routes[0] - 1, 0, half - 1), branches, routes, at, fields, depth, obs_index, obs_value, obs_var
        )
    return by_pieces(at, fields, depth, obs_index, obs_value, obs_var, parent_lookup)


def by_pieces(at, fields, depth, obs_index, obs_value, obs_var, parent_lookup):
    pieces = lax.axis_size("dom")
    n_rows, n_cols = depth.shape
    whole = at * jnp.array([0, 1, 1, 1, 1], jnp.int32)
    (inner,), (inner_h, head, tail) = inner_forecast(whole, fields, depth, 1)
    (outer,), (outer_h,) = outer_forecast(whole, fields, depth, *halo_rows(head, tail), 1)
    misfit_sum = misfit(at, obs_index, obs_value, obs_var, inner_h, outer_h)
    log_weights = log_weight(sum_over(-0.5 * misfit_sum, "rows"))
    slab = jnp.concatenate([outer[:, :HALO], inner, outer[:, HALO:]], axis=1)
    tiles = slab.reshape(3, n_rows, pieces, n_cols // pieces).transpose(2, 0, 1, 3)
    received = lax.all_to_all(tiles, "dom", split_axis=0, concat_axis=0, tiled=True)
    picked = jnp.take(received, parent_lookup, axis=0, mode="clip")
    final = lax.all_to_all(picked, "dom", split_axis=0, concat_axis=0, tiled=True)
    return log_weights, final.transpose(1, 2, 0, 3).reshape(1, 3, n_rows, n_cols)


def solution(mesh):
    in_specs = (P("dom", None, "rows", None), P("rows", None), P(), P(), P(), P())
    out_specs = (P("dom"), P("dom", None, "rows", None))
    return jax.shard_map(shards, mesh=mesh, in_specs=in_specs, out_specs=out_specs, check_vma=False)
```

profile of v0, /device:TPU:0, one launch (start us, length us, event | category | flops | bytes accessed | tf_op | source)
XLA Modules:
  0.0 86.5 jit_solution(556281939107831162)
XLA Ops:
  2.1 83.2 %conditional.1 = (f32[1]{0:T(128)}, f32[1,3,32,4096]{3,2,1,0:T(8,128)}) conditional(s32[]{:T(128)} %bitcast.13, (s32[5]{0:T(128)S(1)}, f32[1,3,32,4096]{3,2,1,0:T(8,128)}, f32[32,4096]{1,0:T(8,128)}, s32[9]{0:T(128)S(1)}, s32[256]{0:T(256)}, /*index=5*/f32[256]{0:T(256)}, f32[256]{0:T(256)}) %tuple.47, ...), branch_computations={%region_0.3_spmd, %region_3.6_spmd, %region_6.9_spmd, %region_9.12... | conditional | flops 110 | bytes 40122616 | solution.py:367
  2.2 5.1 %inner.5 = (f32[3,16,1024]{2,1,0:T(8,128)S(1)}, f32[3,16,1024]{2,1,0:T(8,128)S(1)}, f32[3,16,1024]{2,1,0:T(8,128)S(1)}, f32[3,16,1024]{2,1,0:T(8,128)S(1)}, f32[...) custom-call(s32[5]{0:T(128)S(1)} %get-tuple-element.98.at_ref, ...), custom_call_target="tpu_custom_call" | custom-call | tf_op jit(solution)/shard_map/cond/branch_1_fun/inner/pallas_call | solution.py:90
  7.3 2.4 %collective-permute-start.21 = (f32[4,8,4096]{2,1,0:T(8,128)S(1)}, f32[4,8,4096]{2,1,0:T(8,128)S(1)}, u32[]{:S(2)}, u32[]{:S(2)}) collective-permute-start(f32[4,8,4096]{2,1,0:T(8,128)S(1)} %get-tuple-element.105), channel_id=1, source_target_pairs={{0,1},{1,2},{2,3},{4,5},{5,6},{6,7},{8,9},{9,10},{10,11},{12,13},{... | collective-permute-start | bytes 1572872 | tf_op jit(solution)/shard_map/cond/branch_1_fun/ppermute | solution.py:315
  11.0 2.4 %collective-permute-start.23 = (f32[3,16,1024]{2,1,0:T(8,128)S(1)}, f32[3,16,1024]{2,1,0:T(8,128)S(1)}, u32[]{:S(2)}, u32[]{:S(2)}) collective-permute-start(f32[3,16,1024]{2,1,0:T(8,128)S(1)} %get-tuple-element.110), channel_id=1, source_target_pairs={{0,4},{4,0},{8,12},{12,8},{16,20},{20,16},{24,28},{28,24},{1,5},{5... | collective-permute-start | bytes 589832 | tf_op jit(solution)/shard_map/cond/branch_1_fun/ppermute | solution.py:264
  13.4 1.6 %collective-permute-start.24 = (f32[3,16,1024]{2,1,0:T(8,128)S(1)}, f32[3,16,1024]{2,1,0:T(8,128)S(1)}, u32[]{:S(2)}, u32[]{:S(2)}) collective-permute-start(f32[3,16,1024]{2,1,0:T(8,128)S(1)} %get-tuple-element.111), channel_id=1, source_target_pairs={{0,8},{4,12},{8,0},{12,4},{16,24},{20,28},{24,16},{28,20},{1,9},{5... | collective-permute-start | bytes 589832 | tf_op jit(solution)/shard_map/cond/branch_1_fun/ppermute | solution.py:264
  15.6 5.6 %outer.5 = (f32[3,16,1024]{2,1,0:T(8,128)S(1)}, f32[3,16,1024]{2,1,0:T(8,128)S(1)}, f32[3,16,1024]{2,1,0:T(8,128)S(1)}, f32[3,16,1024]{2,1,0:T(8,128)S(1)}, f32[16,4096]{1,0:T(8,128)S(1)}) custom-call(s32[5]{0:T(128)S(1)} %get-tuple-element.98.at_ref, f32[1,3,32,4096]{3,2,1,0:T(8,128)S(1)} %copy-done.16, f32[32,4096]{1,0:T(8,128)S(1)} %copy-done.20, ...), custom_call_target="tpu_custom_call" | custom-call | tf_op jit(solution)/shard_map/cond/branch_1_fun/outer/pallas_call | solution.py:90
  21.2 1.6 %collective-permute-start.28 = (f32[3,16,1024]{2,1,0:T(8,128)S(1)}, f32[3,16,1024]{2,1,0:T(8,128)S(1)}, u32[]{:S(2)}, u32[]{:S(2)}) collective-permute-start(f32[3,16,1024]{2,1,0:T(8,128)S(1)} %get-tuple-element.114), channel_id=1, source_target_pairs={{0,4},{4,0},{8,12},{12,8},{16,20},{20,16},{24,28},{28,24},{1,5},{5... | collective-permute-start | bytes 589832 | tf_op jit(solution)/shard_map/cond/branch_1_fun/ppermute | solution.py:264
  22.8 1.6 %collective-permute-start.29 = (f32[3,16,1024]{2,1,0:T(8,128)S(1)}, f32[3,16,1024]{2,1,0:T(8,128)S(1)}, u32[]{:S(2)}, u32[]{:S(2)}) collective-permute-start(f32[3,16,1024]{2,1,0:T(8,128)S(1)} %get-tuple-element.115), channel_id=1, source_target_pairs={{0,8},{4,12},{8,0},{12,4},{16,24},{20,28},{24,16},{28,20},{1,9},{5... | collective-permute-start | bytes 589832 | tf_op jit(solution)/shard_map/cond/branch_1_fun/ppermute | solution.py:264
  25.4 2.7 %collective-permute-start.38 = (f32[2,3,16,1024]{3,2,1,0:T(8,128)S(1)}, f32[2,3,16,1024]{3,2,1,0:T(8,128)S(1)}, u32[]{:S(2)}, u32[]{:S(2)}) collective-permute-start(f32[2,3,16,1024]{3,2,1,0:T(8,128)S(1)} %pick.20), channel_id=1, source_target_pairs={{0,16},{4,20},{8,24},{12,28},{16,0},{20,4},{24,8},{28,12},{1,17},{... | collective-permute-start | bytes 1179656 | tf_op jit(solution)/shard_map/cond/branch_1_fun/ppermute | solution.py:264
  28.0 4.5 %misfit.5 = f32[8,128]{1,0:T(8,128)S(1)} custom-call(s32[5]{0:T(128)S(1)} %get-tuple-element.98.at_ref, s32[256]{0:T(256)S(1)} %copy-done.24, f32[256]{0:T(256)S(1)} %copy-done.28, f32[256]{0:T(256)S(1)} %copy-done.32, f32[16,4096]{1,0:T(8,128)S(1)} %get-tuple-element.104.inner_ref, f32[16,4096]{1,0:T(8,128)S(1)} %get-tuple-element.121.outer_ref), custom_call_target="tpu_custom_call" | custom-call | tf_op jit(solution)/shard_map/cond/branch_1_fun/misfit/pallas_call | solution.py:145
  33.7 7.3 %collective-permute-start.26 = (f32[]{:T(128)}, f32[]{:T(128)}, u32[]{:S(2)}, u32[]{:S(2)}) collective-permute-start(f32[]{:T(128)} %bitcast.2), channel_id=1, source_target_pairs={{0,1},{1,0},{2,3},{3,2},{4,5},{5,4},{6,7},{7,6},{8,9},{9,8},{10,11... | collective-permute-start | bytes 20 | tf_op jit(solution)/shard_map/cond/branch_1_fun/ppermute | solution.py:160
  41.5 2.2 %collective-permute-start.27 = (f32[]{:T(128)}, f32[]{:T(128)}, u32[]{:S(2)}, u32[]{:S(2)}) collective-permute-start(f32[]{:T(128)} %add.60), channel_id=1, source_target_pairs={{0,2},{1,3},{2,0},{3,1},{4,6},{5,7},{6,4},{7,5},{8,10},{9,11},{10,... | collective-permute-start | bytes 20 | tf_op jit(solution)/shard_map/cond/branch_1_fun/ppermute | solution.py:160
  46.8 1.5 %collective-permute-start.31 = (f32[8]{0:T(128)S(1)}, f32[8]{0:T(128)S(1)}, u32[]{:S(2)}, u32[]{:S(2)}) collective-permute-start(f32[8]{0:T(128)S(1)} %compare_select_fusion.1), channel_id=1, source_target_pairs={{0,4},{4,0},{8,12},{12,8},{16,20},{20,16},{24,28},{28,24},{1,5},{5... | collective-permute-start | bytes 104 | tf_op jit(solution)/shard_map/cond/branch_1_fun/ppermute | solution.py:160
  48.3 2.0 %collective-permute-done.31 = f32[8]{0:T(128)S(1)} collective-permute-done((f32[8]{0:T(128)S(1)}, f32[8]{0:T(128)S(1)}, u32[]{:S(2)}, u32[]{:S(2)}) %collective-permute-start.31) | collective-permute-done | bytes 64 | tf_op jit(solution)/shard_map/cond/branch_1_fun/ppermute | solution.py:160
  50.3 1.6 %collective-permute-start.32 = (f32[8]{0:T(128)S(1)}, f32[8]{0:T(128)S(1)}, u32[]{:S(2)}, u32[]{:S(2)}) collective-permute-start(f32[8]{0:T(128)S(1)} %fusion.5), channel_id=1, source_target_pairs={{0,8},{4,12},{8,0},{12,4},{16,24},{20,28},{24,16},{28,20},{1,9},{5... | collective-permute-start | bytes 104 | tf_op jit(solution)/shard_map/cond/branch_1_fun/ppermute | solution.py:160
  52.6 1.6 %collective-permute-start.39 = (f32[3,16,1024]{2,1,0:T(8,128)S(1)}, f32[3,16,1024]{2,1,0:T(8,128)S(1)}, u32[]{:S(2)}, u32[]{:S(2)}) collective-permute-start(f32[3,16,1024]{2,1,0:T(8,128)S(1)} %get-tuple-element.133), channel_id=1, source_target_pairs={{0,4},{4,0},{8,12},{12,8},{16,20},{20,16},{24,28},{28,24},{1,5},{5... | collective-permute-start | bytes 589832 | tf_op jit(solution)/shard_map/cond/branch_1_fun/ppermute | solution.py:264
  54.4 4.6 %collective-permute-start.33 = (f32[8]{0:T(128)S(1)}, f32[8]{0:T(128)S(1)}, u32[]{:S(2)}, u32[]{:S(2)}) collective-permute-start(f32[8]{0:T(128)S(1)} %fusion.9), channel_id=1, source_target_pairs={{0,16},{4,20},{8,24},{12,28},{16,0},{20,4},{24,8},{28,12},{1,17},{... | collective-permute-start | bytes 104 | tf_op jit(solution)/shard_map/cond/branch_1_fun/ppermute | solution.py:160
  59.0 3.0 %collective-permute-start.41 = (f32[3,16,1024]{2,1,0:T(8,128)S(1)}, f32[3,16,1024]{2,1,0:T(8,128)S(1)}, u32[]{:S(2)}, u32[]{:S(2)}) collective-permute-start(f32[3,16,1024]{2,1,0:T(8,128)S(1)} %get-tuple-element.135), channel_id=1, source_target_pairs={{0,12},{4,8},{8,4},{12,0},{16,28},{20,24},{24,20},{28,16},{1,13},{... | collective-permute-start | bytes 589832 | tf_op jit(solution)/shard_map/cond/branch_1_fun/ppermute | solution.py:264
  61.9 3.9 %collective-permute-done.34.refs_4_ = f32[2,3,16,1024]{3,2,1,0:T(8,128)S(1)} collective-permute-done((f32[2,3,16,1024]{3,2,1,0:T(8,128)S(1)}, f32[2,3,16,1024]{3,2,1,0:T(8,128)S(1)}, u32[]{:S(2)}, u32[]{:S(2)}) %collective-permute-start.34) | collective-permute-done | bytes 393248 | tf_op jit(solution)/shard_map/cond/branch_1_fun/ppermute | solution.py:264
  66.6 1.6 %collective-permute-start.35 = (f32[3,16,1024]{2,1,0:T(8,128)S(1)}, f32[3,16,1024]{2,1,0:T(8,128)S(1)}, u32[]{:S(2)}, u32[]{:S(2)}) collective-permute-start(f32[3,16,1024]{2,1,0:T(8,128)S(1)} %get-tuple-element.128), channel_id=1, source_target_pairs={{0,4},{4,0},{8,12},{12,8},{16,20},{20,16},{24,28},{28,24},{1,5},{5... | collective-permute-start | bytes 589832 | tf_op jit(solution)/shard_map/cond/branch_1_fun/ppermute | solution.py:264
  68.2 2.0 %collective-permute-start.37 = (f32[3,16,1024]{2,1,0:T(8,128)S(1)}, f32[3,16,1024]{2,1,0:T(8,128)S(1)}, u32[]{:S(2)}, u32[]{:S(2)}) collective-permute-start(f32[3,16,1024]{2,1,0:T(8,128)S(1)} %get-tuple-element.130), channel_id=1, source_target_pairs={{0,12},{4,8},{8,4},{12,0},{16,28},{20,24},{24,20},{28,16},{1,13},{... | collective-permute-start | bytes 589832 | tf_op jit(solution)/shard_map/cond/branch_1_fun/ppermute | solution.py:264
  73.4 2.0 %collective-permute-done.41.refs_3_ = f32[3,16,1024]{2,1,0:T(8,128)S(1)} collective-permute-done((f32[3,16,1024]{2,1,0:T(8,128)S(1)}, f32[3,16,1024]{2,1,0:T(8,128)S(1)}, u32[]{:S(2)}, u32[]{:S(2)}) %collective-permute-start.41) | collective-permute-done | bytes 196640 | tf_op jit(solution)/shard_map/cond/branch_1_fun/ppermute | solution.py:264
  76.8 1.8 %collective-permute-done.36.refs_2_ = f32[3,16,1024]{2,1,0:T(8,128)S(1)} collective-permute-done((f32[3,16,1024]{2,1,0:T(8,128)S(1)}, f32[3,16,1024]{2,1,0:T(8,128)S(1)}, u32[]{:S(2)}, u32[]{:S(2)}) %collective-permute-start.36) | collective-permute-done | bytes 196640 | tf_op jit(solution)/shard_map/cond/branch_1_fun/ppermute | solution.py:264
  78.6 5.1 %collective-permute-done.37.refs_3_ = f32[3,16,1024]{2,1,0:T(8,128)S(1)} collective-permute-done((f32[3,16,1024]{2,1,0:T(8,128)S(1)}, f32[3,16,1024]{2,1,0:T(8,128)S(1)}, u32[]{:S(2)}, u32[]{:S(2)}) %collective-permute-start.37) | collective-permute-done | bytes 196640 | tf_op jit(solution)/shard_map/cond/branch_1_fun/ppermute | solution.py:264
  (46 shorter events, 13.8 us)
Async XLA Ops:
  2.2 13.4 %copy-start.16 = (f32[1,3,32,4096]{3,2,1,0:T(8,128)S(1)}, f32[1,3,32,4096]{3,2,1,0:T(8,128)}, u32[]{:S(2)}) copy-start(f32[1,3,32,4096]{3,2,1,0:T(8,128)} %get-tuple-element.102.fields_ref) | copy-start | bytes 4718596 | tf_op jit(solution)/shard_map/cond
  2.2 13.4 %copy-start.20 = (f32[32,4096]{1,0:T(8,128)S(1)}, f32[32,4096]{1,0:T(8,128)}, u32[]{:S(2)}) copy-start(f32[32,4096]{1,0:T(8,128)} %get-tuple-element.103.depth_ref) | copy-start | bytes 1572868 | tf_op jit(solution)/shard_map/cond
  7.3 7.7 %collective-permute-start.21 = (f32[4,8,4096]{2,1,0:T(8,128)S(1)}, f32[4,8,4096]{2,1,0:T(8,128)S(1)}, u32[]{:S(2)}, u32[]{:S(2)}) collective-permute-start(f32[4,8,4096]{2,1,0:T(8,128)S(1)} %get-tuple-element.105), channel_id=1, source_target_pairs={{0,1},{1,2},{2,3},{4,5},{5,6},{6,7},{8,9},{9,10},{10,11},{12,13},{... | collective-permute-start | bytes 1572872 | tf_op jit(solution)/shard_map/cond/branch_1_fun/ppermute | solution.py:315
  9.7 5.9 %collective-permute-start.22 = (f32[4,8,4096]{2,1,0:T(8,128)S(1)}, f32[4,8,4096]{2,1,0:T(8,128)S(1)}, u32[]{:S(2)}, u32[]{:S(2)}) collective-permute-start(f32[4,8,4096]{2,1,0:T(8,128)S(1)} %get-tuple-element.106), channel_id=1, source_target_pairs={{1,0},{2,1},{3,2},{5,4},{6,5},{7,6},{9,8},{10,9},{11,10},{13,12},{... | collective-permute-start | bytes 1572872 | tf_op jit(solution)/shard_map/cond/branch_1_fun/ppermute | solution.py:316
  11.0 13.4 %collective-permute-start.23 = (f32[3,16,1024]{2,1,0:T(8,128)S(1)}, f32[3,16,1024]{2,1,0:T(8,128)S(1)}, u32[]{:S(2)}, u32[]{:S(2)}) collective-permute-start(f32[3,16,1024]{2,1,0:T(8,128)S(1)} %get-tuple-element.110), channel_id=1, source_target_pairs={{0,4},{4,0},{8,12},{12,8},{16,20},{20,16},{24,28},{28,24},{1,5},{5... | collective-permute-start | bytes 589832 | tf_op jit(solution)/shard_map/cond/branch_1_fun/ppermute | solution.py:264
  13.4 11.4 %collective-permute-start.24 = (f32[3,16,1024]{2,1,0:T(8,128)S(1)}, f32[3,16,1024]{2,1,0:T(8,128)S(1)}, u32[]{:S(2)}, u32[]{:S(2)}) collective-permute-start(f32[3,16,1024]{2,1,0:T(8,128)S(1)} %get-tuple-element.111), channel_id=1, source_target_pairs={{0,8},{4,12},{8,0},{12,4},{16,24},{20,28},{24,16},{28,20},{1,9},{5... | collective-permute-start | bytes 589832 | tf_op jit(solution)/shard_map/cond/branch_1_fun/ppermute | solution.py:264
  15.0 13.1 %copy-start.32 = (f32[256]{0:T(256)S(1)}, f32[256]{0:T(256)}, u32[]{:S(2)}) copy-start(f32[256]{0:T(256)} %get-tuple-element.101.var_ref) | copy-start | bytes 3076 | tf_op jit(solution)/shard_map/cond
  15.0 9.8 %collective-permute-start.25 = (f32[3,16,1024]{2,1,0:T(8,128)S(1)}, f32[3,16,1024]{2,1,0:T(8,128)S(1)}, u32[]{:S(2)}, u32[]{:S(2)}) collective-permute-start(f32[3,16,1024]{2,1,0:T(8,128)S(1)} %get-tuple-element.112), channel_id=1, source_target_pairs={{0,12},{4,8},{8,4},{12,0},{16,28},{20,24},{24,20},{28,16},{1,13},{... | collective-permute-start | bytes 589832 | tf_op jit(solution)/shard_map/cond/branch_1_fun/ppermute | solution.py:264
  21.2 24.5 %collective-permute-start.28 = (f32[3,16,1024]{2,1,0:T(8,128)S(1)}, f32[3,16,1024]{2,1,0:T(8,128)S(1)}, u32[]{:S(2)}, u32[]{:S(2)}) collective-permute-start(f32[3,16,1024]{2,1,0:T(8,128)S(1)} %get-tuple-element.114), channel_id=1, source_target_pairs={{0,4},{4,0},{8,12},{12,8},{16,20},{20,16},{24,28},{28,24},{1,5},{5... | collective-permute-start | bytes 589832 | tf_op jit(solution)/shard_map/cond/branch_1_fun/ppermute | solution.py:264
  22.8 23.0 %collective-permute-start.29 = (f32[3,16,1024]{2,1,0:T(8,128)S(1)}, f32[3,16,1024]{2,1,0:T(8,128)S(1)}, u32[]{:S(2)}, u32[]{:S(2)}) collective-permute-start(f32[3,16,1024]{2,1,0:T(8,128)S(1)} %get-tuple-element.115), channel_id=1, source_target_pairs={{0,8},{4,12},{8,0},{12,4},{16,24},{20,28},{24,16},{28,20},{1,9},{5... | collective-permute-start | bytes 589832 | tf_op jit(solution)/shard_map/cond/branch_1_fun/ppermute | solution.py:264
  24.4 21.4 %collective-permute-start.30 = (f32[3,16,1024]{2,1,0:T(8,128)S(1)}, f32[3,16,1024]{2,1,0:T(8,128)S(1)}, u32[]{:S(2)}, u32[]{:S(2)}) collective-permute-start(f32[3,16,1024]{2,1,0:T(8,128)S(1)} %get-tuple-element.116), channel_id=1, source_target_pairs={{0,12},{4,8},{8,4},{12,0},{16,28},{20,24},{24,20},{28,16},{1,13},{... | collective-permute-start | bytes 589832 | tf_op jit(solution)/shard_map/cond/branch_1_fun/ppermute | solution.py:264
  25.4 26.5 %collective-permute-start.38 = (f32[2,3,16,1024]{3,2,1,0:T(8,128)S(1)}, f32[2,3,16,1024]{3,2,1,0:T(8,128)S(1)}, u32[]{:S(2)}, u32[]{:S(2)}) collective-permute-start(f32[2,3,16,1024]{3,2,1,0:T(8,128)S(1)} %pick.20), channel_id=1, source_target_pairs={{0,16},{4,20},{8,24},{12,28},{16,0},{20,4},{24,8},{28,12},{1,17},{... | collective-permute-start | bytes 1179656 | tf_op jit(solution)/shard_map/cond/branch_1_fun/ppermute | solution.py:264
  33.7 7.3 %collective-permute-start.26 = (f32[]{:T(128)}, f32[]{:T(128)}, u32[]{:S(2)}, u32[]{:S(2)}) collective-permute-start(f32[]{:T(128)} %bitcast.2), channel_id=1, source_target_pairs={{0,1},{1,0},{2,3},{3,2},{4,5},{5,4},{6,7},{7,6},{8,9},{9,8},{10,11... | collective-permute-start | bytes 20 | tf_op jit(solution)/shard_map/cond/branch_1_fun/ppermute | solution.py:160
  41.5 3.7 %collective-permute-start.27 = (f32[]{:T(128)}, f32[]{:T(128)}, u32[]{:S(2)}, u32[]{:S(2)}) collective-permute-start(f32[]{:T(128)} %add.60), channel_id=1, source_target_pairs={{0,2},{1,3},{2,0},{3,1},{4,6},{5,7},{6,4},{7,5},{8,10},{9,11},{10,... | collective-permute-start | bytes 20 | tf_op jit(solution)/shard_map/cond/branch_1_fun/ppermute | solution.py:160
  46.4 19.5 %collective-permute-start.34 = (f32[2,3,16,1024]{3,2,1,0:T(8,128)S(1)}, f32[2,3,16,1024]{3,2,1,0:T(8,128)S(1)}, u32[]{:S(2)}, u32[]{:S(2)}) collective-permute-start(f32[2,3,16,1024]{3,2,1,0:T(8,128)S(1)} %pick.21), channel_id=1, source_target_pairs={{0,16},{4,20},{8,24},{12,28},{16,0},{20,4},{24,8},{28,12},{1,17},{... | collective-permute-start | bytes 1179656 | tf_op jit(solution)/shard_map/cond/branch_1_fun/ppermute | solution.py:264
  46.8 3.5 %collective-permute-start.31 = (f32[8]{0:T(128)S(1)}, f32[8]{0:T(128)S(1)}, u32[]{:S(2)}, u32[]{:S(2)}) collective-permute-start(f32[8]{0:T(128)S(1)} %compare_select_fusion.1), channel_id=1, source_target_pairs={{0,4},{4,0},{8,12},{12,8},{16,20},{20,16},{24,28},{28,24},{1,5},{5... | collective-permute-start | bytes 104 | tf_op jit(solution)/shard_map/cond/branch_1_fun/ppermute | solution.py:160
  50.3 4.1 %collective-permute-start.32 = (f32[8]{0:T(128)S(1)}, f32[8]{0:T(128)S(1)}, u32[]{:S(2)}, u32[]{:S(2)}) collective-permute-start(f32[8]{0:T(128)S(1)} %fusion.5), channel_id=1, source_target_pairs={{0,8},{4,12},{8,0},{12,4},{16,24},{20,28},{24,16},{28,20},{1,9},{5... | collective-permute-start | bytes 104 | tf_op jit(solution)/shard_map/cond/branch_1_fun/ppermute | solution.py:160
  52.6 15.6 %collective-permute-start.39 = (f32[3,16,1024]{2,1,0:T(8,128)S(1)}, f32[3,16,1024]{2,1,0:T(8,128)S(1)}, u32[]{:S(2)}, u32[]{:S(2)}) collective-permute-start(f32[3,16,1024]{2,1,0:T(8,128)S(1)} %get-tuple-element.133), channel_id=1, source_target_pairs={{0,4},{4,0},{8,12},{12,8},{16,20},{20,16},{24,28},{28,24},{1,5},{5... | collective-permute-start | bytes 589832 | tf_op jit(solution)/shard_map/cond/branch_1_fun/ppermute | solution.py:264
  54.4 13.8 %collective-permute-start.33 = (f32[8]{0:T(128)S(1)}, f32[8]{0:T(128)S(1)}, u32[]{:S(2)}, u32[]{:S(2)}) collective-permute-start(f32[8]{0:T(128)S(1)} %fusion.9), channel_id=1, source_target_pairs={{0,16},{4,20},{8,24},{12,28},{16,0},{20,4},{24,8},{28,12},{1,17},{... | collective-permute-start | bytes 104 | tf_op jit(solution)/shard_map/cond/branch_1_fun/ppermute | solution.py:160
  59.0 14.4 %collective-permute-start.40 = (f32[3,16,1024]{2,1,0:T(8,128)S(1)}, f32[3,16,1024]{2,1,0:T(8,128)S(1)}, u32[]{:S(2)}, u32[]{:S(2)}) collective-permute-start(f32[3,16,1024]{2,1,0:T(8,128)S(1)} %get-tuple-element.134), channel_id=1, source_target_pairs={{0,8},{4,12},{8,0},{12,4},{16,24},{20,28},{24,16},{28,20},{1,9},{5... | collective-permute-start | bytes 589832 | tf_op jit(solution)/shard_map/cond/branch_1_fun/ppermute | solution.py:264
  59.0 16.4 %collective-permute-start.41 = (f32[3,16,1024]{2,1,0:T(8,128)S(1)}, f32[3,16,1024]{2,1,0:T(8,128)S(1)}, u32[]{:S(2)}, u32[]{:S(2)}) collective-permute-start(f32[3,16,1024]{2,1,0:T(8,128)S(1)} %get-tuple-element.135), channel_id=1, source_target_pairs={{0,12},{4,8},{8,4},{12,0},{16,28},{20,24},{24,20},{28,16},{1,13},{... | collective-permute-start | bytes 589832 | tf_op jit(solution)/shard_map/cond/branch_1_fun/ppermute | solution.py:264
  66.6 10.2 %collective-permute-start.35 = (f32[3,16,1024]{2,1,0:T(8,128)S(1)}, f32[3,16,1024]{2,1,0:T(8,128)S(1)}, u32[]{:S(2)}, u32[]{:S(2)}) collective-permute-start(f32[3,16,1024]{2,1,0:T(8,128)S(1)} %get-tuple-element.128), channel_id=1, source_target_pairs={{0,4},{4,0},{8,12},{12,8},{16,20},{20,16},{24,28},{28,24},{1,5},{5... | collective-permute-start | bytes 589832 | tf_op jit(solution)/shard_map/cond/branch_1_fun/ppermute | solution.py:264
  68.2 10.4 %collective-permute-start.36 = (f32[3,16,1024]{2,1,0:T(8,128)S(1)}, f32[3,16,1024]{2,1,0:T(8,128)S(1)}, u32[]{:S(2)}, u32[]{:S(2)}) collective-permute-start(f32[3,16,1024]{2,1,0:T(8,128)S(1)} %get-tuple-element.129), channel_id=1, source_target_pairs={{0,8},{4,12},{8,0},{12,4},{16,24},{20,28},{24,16},{28,20},{1,9},{5... | collective-permute-start | bytes 589832 | tf_op jit(solution)/shard_map/cond/branch_1_fun/ppermute | solution.py:264
  68.2 15.5 %collective-permute-start.37 = (f32[3,16,1024]{2,1,0:T(8,128)S(1)}, f32[3,16,1024]{2,1,0:T(8,128)S(1)}, u32[]{:S(2)}, u32[]{:S(2)}) collective-permute-start(f32[3,16,1024]{2,1,0:T(8,128)S(1)} %get-tuple-element.130), channel_id=1, source_target_pairs={{0,12},{4,8},{8,4},{12,0},{16,28},{20,24},{24,20},{28,16},{1,13},{... | collective-permute-start | bytes 589832 | tf_op jit(solution)/shard_map/cond/branch_1_fun/ppermute | solution.py:264
  (2 other events, 26.1 us)
where the time goes:
time: 86.7 us; the launch traced here: 86.5 us
  starting transfers between devices  39.5 us (46%)
  Pallas kernels  22.1 us (25%)
  waiting for transfers between devices  17.1 us (20%)
  loops' own time  3.48 us (4%)
  other arithmetic  1.86 us (2%)
  between operations  1.84 us (2%)
    ppermute x14, starting transfers between devices, to_mate(): lax.ppermute(x, 'dom', [(i, i ^ m) for i in range(lax.axis_size('dom'))])  18.7 us
    ppermute x5, starting transfers between devices, sum_over(): x = x + lax.ppermute(x, axis, [(i, i ^ step) for i in range(count)])  17.1 us
    ppermute x14, waiting for transfers between devices, to_mate(): lax.ppermute(x, 'dom', [(i, i ^ m) for i in range(lax.axis_size('dom'))])  12.8 us
    pallas_call x2, Pallas kernels, forecast(): pl.pallas_call(kernel, out_shape=[jax.ShapeDtypeStruct(shape, jnp.float32...  10.7 us
    pallas_call x1, Pallas kernels, misfit(): pl.pallas_call(misfit_kernel, out_shape=jax.ShapeDtypeStruct((8, LANES),...  4.45 us
    ppermute x5, waiting for transfers between devices, sum_over(): x = x + lax.ppermute(x, axis, [(i, i ^ step) for i in range(count)])  3.73 us
    another operation x1, loops' own time, shards(): lax.switch(jnp.clip(routes[0] - 1, 0, half - 1), branches, routes, at, fi...  3.48 us
    pallas_call x2, Pallas kernels, place(): pl.pallas_call(kernel, out_shape=pltpu.HBM(shape, jnp.float32), in_specs=...  2.93 us
  transfers between devices with their start and end apart: 21, of which 8 were waited for; matrix products, arithmetic and copies ran while one was open for 3% of the time, Pallas kernels for 16%

commit v1 on v0

--- a/solution.py
+++ b/solution.py
@@ -9,6 +9,7 @@
 HALO = 2 * STEPS
 LANES = 128
 VMEM_BYTES = 48 * 2**20
+ROUTED_HALF = 4
 
 time_step = 0.5
 coriolis = 0.2
@@ -57,13 +58,10 @@
 
 
 def inner_kernel(at_ref, fields_ref, depth_ref, *refs):
-    outs, (h_ref, head_ref, tail_ref), state = refs[:-7], refs[-7:-4], refs[-4:]
+    outs, h_ref, state = refs[:-5], refs[-5], refs[-4:]
     n_rows = depth_ref.shape[0]
     for k in range(4):
-        field = depth_ref[...] if k == 3 else fields_ref[0, k]
-        state[k][...] = field
-        head_ref[k] = field[:HALO]
-        tail_ref[k] = field[n_rows - HALO :]
+        state[k][...] = depth_ref[...] if k == 3 else fields_ref[0, k]
     model_steps(*state)
     h_ref[...] = state[0][HALO : n_rows - HALO]
     store_pieces(at_ref, outs, state, lambda ref, at: ref[HALO : n_rows - HALO, at])
@@ -85,8 +83,8 @@
     store_pieces(at_ref, outs, state, outer_rows)
 
 
-def forecast(kernel, name, at, arrays, n_rows, n_cols, count, window_rows, extra=()):
-    shapes = [(3, n_rows, n_cols // count)] * count + [(n_rows, n_cols)] + list(extra)
+def forecast(kernel, name, at, arrays, n_rows, n_cols, count, window_rows):
+    shapes = [(3, n_rows, n_cols // count)] * count + [(n_rows, n_cols)]
     outs = pl.pallas_call(
         kernel,
         out_shape=[jax.ShapeDtypeStruct(shape, jnp.float32) for shape in shapes],
@@ -96,7 +94,7 @@
         compiler_params=pltpu.CompilerParams(vmem_limit_bytes=VMEM_BYTES),
         name=name,
     )(at, *arrays)
-    return list(outs[:count]), outs[count:]
+    return list(outs[:count]), outs[count]
 
 
 def misfit_kernel(at_ref, index_ref, value_ref, var_ref, inner_ref, outer_ref, out_ref, total_ref):
@@ -138,19 +136,20 @@
 
     total_ref[...] = jnp.zeros_like(total_ref)
     lax.fori_loop(0, index_ref.shape[0], point, 0, unroll=8)
-    out_ref[...] = jnp.broadcast_to(jnp.sum(total_ref[...]), out_ref.shape)
+    lane = lax.broadcasted_iota(jnp.int32, out_ref.shape, 1)
+    out_ref[...] = jnp.where(lane == at_ref[5], -0.5 * jnp.sum(total_ref[...]), 0.0)
 
 
 def misfit(at, obs_index, obs_value, obs_var, inner, outer):
     return pl.pallas_call(
         misfit_kernel,
-        out_shape=jax.ShapeDtypeStruct((8, LANES), jnp.float32),
+        out_shape=jax.ShapeDtypeStruct((1, LANES), jnp.float32),
         in_specs=[in_smem] * 4 + [in_vmem] * 2,
         out_specs=in_vmem,
         scratch_shapes=[pltpu.VMEM((8, LANES), jnp.float32)],
         compiler_params=pltpu.CompilerParams(vmem_limit_bytes=VMEM_BYTES),
         name="misfit",
-    )(at, obs_index, obs_value, obs_var, inner, outer)[0, 0]
+    )(at, obs_index, obs_value, obs_var, inner, outer)
 
 
 def sum_over(x, axis):
@@ -162,12 +161,23 @@
     return x
 
 
-def log_weight(loglik):
-    slots = lax.broadcasted_iota(jnp.int32, (lax.axis_size("dom"),), 0)
-    every = sum_over(jnp.where(slots == lax.axis_index("dom"), loglik, 0.0), "dom")
-    peak = jnp.max(every)
-    total = jnp.sum(jnp.exp(every - peak))
-    return (loglik - (peak + jnp.log(total)))[None]
+def weigh_kernel(at_ref, loglik_ref, out_ref, *, particles):
+    lane = lax.broadcasted_iota(jnp.int32, loglik_ref.shape, 1)
+    loglik = loglik_ref[...]
+    peak = jnp.max(jnp.where(lane < particles, loglik, -jnp.inf), axis=1, keepdims=True)
+    total = jnp.sum(jnp.where(lane < particles, jnp.exp(loglik - peak), 0.0), axis=1, keepdims=True)
+    out_ref[0] = jnp.sum(jnp.where(lane == at_ref[5], loglik - (peak + jnp.log(total)), 0.0))
+
+
+def log_weight(at, loglik):
+    particles = lax.axis_size("dom")
+    return pl.pallas_call(
+        lambda *refs: weigh_kernel(*refs, particles=particles),
+        out_shape=jax.ShapeDtypeStruct((1,), jnp.float32),
+        in_specs=[in_smem, in_vmem],
+        out_specs=in_smem,
+        name="weigh",
+    )(at, loglik)
 
 
 def place(at, pieces, spans, shape, into=None):
@@ -207,7 +217,22 @@
     )(at, *pieces, *extra)
 
 
-def route_kernel(at_ref, parents_ref, out_ref, *, half):
+def prepare_kernel(at_ref, parents_ref, fields_ref, depth_ref, routes_ref, head_ref, tail_ref, sems, *, half):
+    n_rows = depth_ref.shape[0]
+    copies = []
+    for ref, first in ((head_ref, 0), (tail_ref, n_rows - HALO)):
+        rows = pl.ds(first, HALO)
+        copies.append(pltpu.make_async_copy(fields_ref.at[0, :, rows], ref.at[pl.ds(0, 3)], sems.at[len(copies)]))
+        copies.append(pltpu.make_async_copy(depth_ref.at[rows], ref.at[3], sems.at[len(copies)]))
+    for c in copies:
+        c.start()
+    if half <= ROUTED_HALF:
+        route(at_ref, parents_ref, routes_ref, half)
+    for c in copies:
+        c.wait()
+
+
+def route(at_ref, parents_ref, out_ref, half):
     own = at_ref[0]
     side = at_ref[4]
     parents = [parents_ref[s] for s in range(2 * half)]
@@ -250,14 +275,18 @@
         out_ref[1 + half + m] = jnp.where(is_local, jnp.bitwise_xor(local, own), half + from_rank)
 
 
-def route(at, parent_lookup, half):
+def prepare(at, parent_lookup, fields, depth, half):
+    n_rows, n_cols = depth.shape
+    rim = jax.ShapeDtypeStruct((4, HALO, n_cols), jnp.float32)
     return pl.pallas_call(
-        lambda *refs: route_kernel(*refs, half=half),
-        out_shape=jax.ShapeDtypeStruct((1 + 2 * half,), jnp.int32),
-        in_specs=[in_smem, in_smem],
-        out_specs=in_smem,
-        name="route",
-    )(at, parent_lookup)
+        lambda *refs: prepare_kernel(*refs, half=half),
+        out_shape=[jax.ShapeDtypeStruct((1 + 2 * half,), jnp.int32), rim, rim],
+        in_specs=[in_smem, in_smem, in_hbm, in_hbm],
+        out_specs=[in_smem, in_vmem, in_vmem],
+        scratch_shapes=[pltpu.SemaphoreType.DMA((4,))],
+        compiler_params=pltpu.CompilerParams(vmem_limit_bytes=VMEM_BYTES),
+        name="prepare",
+    )(at, parent_lookup, fields, depth)
 
 
 def to_mate(x, m):
@@ -268,7 +297,7 @@
     return [x if m == 0 else to_mate(x, m) for m, x in enumerate(pieces)]
 
 
-def pick(routes, first, count, sources, stacks=(), stacked=False):
+def pick(routes, first, count, sources, stacks=(), stacked=False, cost=None):
     block = sources[0].shape
 
     def kernel(routes_ref, *refs):
@@ -294,12 +323,13 @@
         in_specs=[in_smem] + [in_vmem] * (len(sources) + len(stacks)),
         out_specs=[in_vmem] * len(shapes),
         compiler_params=pltpu.CompilerParams(vmem_limit_bytes=VMEM_BYTES),
+        cost_estimate=cost,
         name="pick",
     )(routes, *sources, *stacks)
 
 
-def chosen(held, routes, crossing):
-    return pick(routes, 1, crossing, held, stacked=True)[0]
+def chosen(held, routes, crossing, cost=None):
+    return pick(routes, 1, crossing, held, stacked=True, cost=cost)[0]
 
 
 def for_slots(held, got, routes):
@@ -319,8 +349,7 @@
 
 def inner_forecast(at, fields, depth, count):
     n_rows, n_cols = depth.shape
-    rim = (4, HALO, n_cols)
-    return forecast(inner_kernel, "inner", at, (fields, depth), n_rows - 2 * HALO, n_cols, count, n_rows, (rim, rim))
+    return forecast(inner_kernel, "inner", at, (fields, depth), n_rows - 2 * HALO, n_cols, count, n_rows)
 
 
 def outer_forecast(at, fields, depth, above, below, count):
@@ -329,24 +358,28 @@
     return forecast(outer_kernel, "outer", at, arrays, 2 * HALO, n_cols, count, n_rows + 2 * HALO)
 
 
-def cycle(crossing, routes, at, fields, depth, obs_index, obs_value, obs_var):
+def cycle(crossing, routes, head, tail, at, fields, depth, obs_index, obs_value, obs_var):
     half = lax.axis_size("dom") // 2
     n_rows, n_cols = depth.shape
-    inner, (inner_h, head, tail) = inner_forecast(at, fields, depth, half)
     above, below = halo_rows(head, tail)
+    inner, inner_h = inner_forecast(at, fields, depth, half)
     inner_held = among_mates(inner)
-    outer, (outer_h,) = outer_forecast(at, fields, depth, above, below, half)
+    outer, outer_h = outer_forecast(at, fields, depth, above, below, half)
     outer_held = among_mates(outer)
     inner_chosen = chosen(after(inner_held, outer), routes, crossing)
     inner_got = to_mate(inner_chosen, half)
-    misfit_sum = misfit(at, obs_index, obs_value, obs_var, inner_h, after(outer_h, inner_chosen))
-    loglik = sum_over(-0.5 * misfit_sum, "rows")
+    loglik = misfit(at, obs_index, obs_value, obs_var, inner_h, after(outer_h, inner_chosen))
+    step = 1
+    while step < half:
+        loglik = loglik + to_mate(loglik, step)
+        step *= 2
     outer_chosen = chosen(after(outer_held, loglik), routes, crossing)
     outer_got = to_mate(outer_chosen, half)
+    loglik = loglik + to_mate(loglik, half)
     inner_done = among_mates(for_slots(inner_held, after(inner_got, outer_chosen), routes))
-    log_weights = log_weight(after(loglik, outer_chosen))
     outer_slots = for_slots(outer_held, outer_got, routes)
     outer_done = among_mates(outer_slots)
+    log_weights = log_weight(at, sum_over(after(loglik, outer_slots), "rows"))
     members = place(at, after(inner_done, outer_slots), ((0, HALO, n_rows - 2 * HALO),), fields.shape)
     members = place(at, outer_done, ((0, 0, HALO), (HALO, n_rows - HALO, HALO)), fields.shape, members)
     return log_weights, members
@@ -357,27 +390,24 @@
     dom_at = lax.axis_index("dom")
     half = lax.axis_size("dom") // 2
     at = jnp.stack(
-        [dom_at % half, rows_at > 0, rows_at < lax.axis_size("rows") - 1, rows_at, dom_at // half]
+        [dom_at % half, rows_at > 0, rows_at < lax.axis_size("rows") - 1, rows_at, dom_at // half, dom_at]
     ).astype(jnp.int32)
-    if half == 4:
-        routes = route(at, parent_lookup, half)
-        branches = [
-            (lambda r, a, *rest, c=c: cycle(c, r, a, *rest)) for c in range(1, half + 1)
-        ]
-        return lax.switch(
-            jnp.clip(routes[0] - 1, 0, half - 1), branches, routes, at, fields, depth, obs_index, obs_value, obs_var
-        )
-    return by_pieces(at, fields, depth, obs_index, obs_value, obs_var, parent_lookup)
-
-
-def by_pieces(at, fields, depth, obs_index, obs_value, obs_var, parent_lookup):
+    routes, head, tail = prepare(at, parent_lookup, fields, depth, half)
+    if half == ROUTED_HALF:
+        branches = [(lambda *rest, c=c: cycle(c, *rest)) for c in range(1, half + 1)]
+        crossing = jnp.clip(routes[0] - 1, 0, half - 1)
+        return lax.switch(crossing, branches, routes, head, tail, at, fields, depth, obs_index, obs_value, obs_var)
+    return by_pieces(head, tail, at, fields, depth, obs_index, obs_value, obs_var, parent_lookup)
+
+
+def by_pieces(head, tail, at, fields, depth, obs_index, obs_value, obs_var, parent_lookup):
     pieces = lax.axis_size("dom")
     n_rows, n_cols = depth.shape
-    whole = at * jnp.array([0, 1, 1, 1, 1], jnp.int32)
-    (inner,), (inner_h, head, tail) = inner_forecast(whole, fields, depth, 1)
-    (outer,), (outer_h,) = outer_forecast(whole, fields, depth, *halo_rows(head, tail), 1)
-    misfit_sum = misfit(at, obs_index, obs_value, obs_var, inner_h, outer_h)
-    log_weights = log_weight(sum_over(-0.5 * misfit_sum, "rows"))
+    whole = at * jnp.array([0, 1, 1, 1, 1, 1], jnp.int32)
+    (inner,), inner_h = inner_forecast(whole, fields, depth, 1)
+    (outer,), outer_h = outer_forecast(whole, fields, depth, *halo_rows(head, tail), 1)
+    loglik = misfit(at, obs_index, obs_value, obs_var, inner_h, outer_h)
+    log_weights = log_weight(at, sum_over(sum_over(loglik, "dom"), "rows"))
     slab = jnp.concatenate([outer[:, :HALO], inner, outer[:, HALO:]], axis=1)
     tiles = slab.reshape(3, n_rows, pieces, n_cols // pieces).transpose(2, 0, 1, 3)
     received = lax.all_to_all(tiles, "dom", split_axis=0, concat_axis=0, tiled=True)

time: 86.7 us -> 86.1 us (level)
  waiting for transfers between devices: 17.1 us -> 27.3 us
  starting transfers between devices: 39.5 us -> 31.9 us
  loops' own time: 3.48 us -> 0.44 us
  Pallas kernels: 22.1 us -> 23.9 us
  other arithmetic: 1.86 us -> 0.59 us
  between operations: 1.84 us -> 0.97 us
    ppermute x5 -> x2, starting transfers between devices: 17.1 us -> 2.39 us  [sum_over(): x = x + lax.ppermute(x, axis, [(i, i ^ step) for i in range(count)])]
    ppermute x14 -> x17, waiting for transfers between devices: 12.8 us -> 27.3 us  [to_mate(): lax.ppermute(x, 'dom', [(i, i ^ m) for i in range(lax.axis_size('dom'))])]
    ppermute x14 -> x17, starting transfers between devices: 18.7 us -> 25.9 us  [to_mate(): lax.ppermute(x, 'dom', [(i, i ^ m) for i in range(lax.axis_size('dom'))])]
    ppermute x5 -> x2, waiting for transfers between devices: 3.73 us -> 0.01 us  [sum_over(): x = x + lax.ppermute(x, axis, [(i, i ^ step) for i in range(count)])]
    another operation x1, loops' own time: 3.48 us -> 0.44 us  [shards(): lax.switch(crossing, branches, routes, head, tail, at, fields, depth, obs...]
    pallas_call x2 -> x3, Pallas kernels: 5.8 us -> 8.84 us  [the longest x1 4.52 us: misfit(): pl.pallas_call(misfit_kernel, out_shape=jax.ShapeDtypeStruct((1, LANES),...]
    reduce_sum x1 -> x0, other arithmetic: 1.25 us -> none  [log_weight(): total = jnp.sum(jnp.exp(every - peak))]
    pallas_call x2, Pallas kernels: 10.7 us -> 9.49 us  [forecast(): pl.pallas_call(kernel, out_shape=[jax.ShapeDtypeStruct(shape, jnp.float32...]
  transfers between devices with their start and end apart: 21 -> 21, of which waited for: 8 -> 6; matrix products, arithmetic and copies ran while one was open for 3% -> 1% of each run, Pallas kernels for 16% -> 23%
where the time goes in v1:
time: 86.1 us; the launch traced here: 85.9 us
  starting transfers between devices  31.9 us (37%)
  waiting for transfers between devices  27.3 us (32%)
  Pallas kernels  23.9 us (28%)
  between operations  0.97 us (1%)
    ppermute x17, waiting for transfers between devices, to_mate(): lax.ppermute(x, 'dom', [(i, i ^ m) for i in range(lax.axis_size('dom'))])  27.3 us
    ppermute x17, starting transfers between devices, to_mate(): lax.ppermute(x, 'dom', [(i, i ^ m) for i in range(lax.axis_size('dom'))])  25.9 us
    pallas_call x2, Pallas kernels, forecast(): pl.pallas_call(kernel, out_shape=[jax.ShapeDtypeStruct(shape, jnp.float32...  9.49 us
    pallas_call x1, Pallas kernels, misfit(): pl.pallas_call(misfit_kernel, out_shape=jax.ShapeDtypeStruct((1, LANES),...  4.52 us
    pallas_call x2, Pallas kernels, place(): pl.pallas_call(kernel, out_shape=pltpu.HBM(shape, jnp.float32), in_specs=...  2.93 us
    pallas_call x1, Pallas kernels, prepare(): pl.pallas_call(lambda *refs: prepare_kernel(*refs, half=half), out_shape=...  2.85 us
    pallas_call x4, Pallas kernels, pick(): pl.pallas_call(kernel, out_shape=[jax.ShapeDtypeStruct(shape, jnp.float32...  2.61 us
    ppermute x1, starting transfers between devices, halo_rows(): above = lax.ppermute(tail, 'rows', [(i, i + 1) for i in range(count - 1)])  2.39 us
  transfers between devices with their start and end apart: 21, of which 6 were waited for; matrix products, arithmetic and copies ran while one was open for 1% of the time, Pallas kernels for 23%

profile of v1, /device:TPU:0, one launch (start us, length us, event | category | flops | bytes accessed | tf_op | source)
XLA Modules:
  0.0 85.9 jit_solution(10914160388502303035)
XLA Ops:
  1.4 2.8 %prepare.1 = (s32[9]{0:T(128)S(1)}, f32[4,8,4096]{2,1,0:T(8,128)}, f32[4,8,4096]{2,1,0:T(8,128)}) custom-call(s32[6]{0:T(128)S(1)} %stack.35.refs_0_, s32[8]{0:T(128)S(1)} %copy-done, f32[1,3,32,4096]{3,2,1,0:T(8,128)} %refs_2_.1, f32[32,4096]{1,0:T(8,128)} %refs_3_.1), custom_call_target="tpu_custom_call" | custom-call | tf_op jit(solution)/shard_map/prepare/pallas_call | solution.py:281
  4.4 81.3 %conditional.1 = (f32[1]{0:T(128)}, f32[1,3,32,4096]{3,2,1,0:T(8,128)}) conditional(s32[]{:T(128)} %bitcast.6, (s32[6]{0:T(128)S(1)}, f32[1,3,32,4096]{3,2,1,0:T(8,128)S(1)}, f32[32,4096]{1,0:T(8,128)S(1)}, f32[4,8,4096]{2,1,0:T(8,128)}, f32[4,8,4096]{2,1,0:T(8,128)}, /*index=5*/s32[9]{0:T(128)S(1)}, ...), branch_computations={%region_0.1_spmd, %region_1.2_spmd, %region_2.3_spmd, %region_3.4_... | conditional | flops 640 | bytes 19941720 | solution.py:399
  4.4 2.4 %collective-permute-start.21 = (f32[4,8,4096]{2,1,0:T(8,128)}, f32[4,8,4096]{2,1,0:T(8,128)S(1)}, u32[]{:S(2)}, u32[]{:S(2)}) collective-permute-start(f32[4,8,4096]{2,1,0:T(8,128)} %get-tuple-element.121), channel_id=1, source_target_pairs={{0,1},{1,2},{2,3},{4,5},{5,6},{6,7},{8,9},{9,10},{10,11},{12,13},{... | collective-permute-start | bytes 1572872 | tf_op jit(solution)/shard_map/cond/branch_1_fun/ppermute | solution.py:345
  8.1 3.9 %inner.5 = (f32[3,16,1024]{2,1,0:T(8,128)S(1)}, f32[3,16,1024]{2,1,0:T(8,128)S(1)}, f32[3,16,1024]{2,1,0:T(8,128)S(1)}, f32[3,16,1024]{2,1,0:T(8,128)S(1)}, f32[16,4096]{1,0:T(8,128)S(1)}) custom-call(s32[6]{0:T(128)S(1)} %get-tuple-element.114.at_ref.refs_0_, f32[1,3,32,4096]{3,2,1,0:T(8,128)S(1)} %get-tuple-element.118.fields_ref, ...), custom_call_target="tpu_custom_call" | custom-call | tf_op jit(solution)/shard_map/cond/branch_1_fun/inner/pallas_call | solution.py:88
  12.0 2.4 %collective-permute-start.23 = (f32[3,16,1024]{2,1,0:T(8,128)S(1)}, f32[3,16,1024]{2,1,0:T(8,128)S(1)}, u32[]{:S(2)}, u32[]{:S(2)}) collective-permute-start(f32[3,16,1024]{2,1,0:T(8,128)S(1)} %get-tuple-element.126), channel_id=1, source_target_pairs={{0,4},{4,0},{8,12},{12,8},{16,20},{20,16},{24,28},{28,24},{1,5},{5... | collective-permute-start | bytes 589832 | tf_op jit(solution)/shard_map/cond/branch_1_fun/ppermute | solution.py:293
  14.4 1.6 %collective-permute-start.24 = (f32[3,16,1024]{2,1,0:T(8,128)S(1)}, f32[3,16,1024]{2,1,0:T(8,128)S(1)}, u32[]{:S(2)}, u32[]{:S(2)}) collective-permute-start(f32[3,16,1024]{2,1,0:T(8,128)S(1)} %get-tuple-element.127), channel_id=1, source_target_pairs={{0,8},{4,12},{8,0},{12,4},{16,24},{20,28},{24,16},{28,20},{1,9},{5... | collective-permute-start | bytes 589832 | tf_op jit(solution)/shard_map/cond/branch_1_fun/ppermute | solution.py:293
  16.0 5.6 %outer.5 = (f32[3,16,1024]{2,1,0:T(8,128)S(1)}, f32[3,16,1024]{2,1,0:T(8,128)S(1)}, f32[3,16,1024]{2,1,0:T(8,128)S(1)}, f32[3,16,1024]{2,1,0:T(8,128)S(1)}, f32[16,4096]{1,0:T(8,128)S(1)}) custom-call(s32[6]{0:T(128)S(1)} %get-tuple-element.114.at_ref.refs_0_, f32[1,3,32,4096]{3,2,1,0:T(8,128)S(1)} %get-tuple-element.118.fields_ref, ...), custom_call_target="tpu_custom_call" | custom-call | tf_op jit(solution)/shard_map/cond/branch_1_fun/outer/pallas_call | solution.py:88
  21.6 2.0 %collective-permute-start.29 = (f32[3,16,1024]{2,1,0:T(8,128)S(1)}, f32[3,16,1024]{2,1,0:T(8,128)S(1)}, u32[]{:S(2)}, u32[]{:S(2)}) collective-permute-start(f32[3,16,1024]{2,1,0:T(8,128)S(1)} %get-tuple-element.130), channel_id=1, source_target_pairs={{0,4},{4,0},{8,12},{12,8},{16,20},{20,16},{24,28},{28,24},{1,5},{5... | collective-permute-start | bytes 589832 | tf_op jit(solution)/shard_map/cond/branch_1_fun/ppermute | solution.py:293
  23.6 1.6 %collective-permute-start.30 = (f32[3,16,1024]{2,1,0:T(8,128)S(1)}, f32[3,16,1024]{2,1,0:T(8,128)S(1)}, u32[]{:S(2)}, u32[]{:S(2)}) collective-permute-start(f32[3,16,1024]{2,1,0:T(8,128)S(1)} %get-tuple-element.131), channel_id=1, source_target_pairs={{0,8},{4,12},{8,0},{12,4},{16,24},{20,28},{24,16},{28,20},{1,9},{5... | collective-permute-start | bytes 589832 | tf_op jit(solution)/shard_map/cond/branch_1_fun/ppermute | solution.py:293
  25.8 3.0 %collective-permute-start.38 = (f32[2,3,16,1024]{3,2,1,0:T(8,128)S(1)}, f32[2,3,16,1024]{3,2,1,0:T(8,128)S(1)}, u32[]{:S(2)}, u32[]{:S(2)}) collective-permute-start(f32[2,3,16,1024]{3,2,1,0:T(8,128)S(1)} %pick.20), channel_id=1, source_target_pairs={{0,16},{4,20},{8,24},{12,28},{16,0},{20,4},{24,8},{28,12},{1,17},{... | collective-permute-start | bytes 1179656 | tf_op jit(solution)/shard_map/cond/branch_1_fun/ppermute | solution.py:293
  28.8 4.5 %misfit.5 = f32[1,128]{1,0:T(1,128)S(1)} custom-call(s32[6]{0:T(128)S(1)} %get-tuple-element.114.at_ref.refs_0_, s32[256]{0:T(256)S(1)} %get-tuple-element.115.index_ref, f32[256]{0:T(256)S(1)} %get-tuple-element.116.value_ref, f32[256]{0:T(256)S(1)} %get-tuple-element.117.var_ref, f32[16,4096]{1,0:T(8,128)S(1)} %get-tuple-element.120.inner_ref, ...), custom_call_target="tpu_custom_call" | custom-call | tf_op jit(solution)/shard_map/cond/branch_1_fun/misfit/pallas_call | solution.py:144
  33.3 1.6 %collective-permute-start.26 = (f32[1,128]{1,0:T(1,128)S(1)}, f32[1,128]{1,0:T(1,128)S(1)}, u32[]{:S(2)}, u32[]{:S(2)}) collective-permute-start(f32[1,128]{1,0:T(1,128)S(1)} %misfit.5), channel_id=1, source_target_pairs={{0,4},{4,0},{8,12},{12,8},{16,20},{20,16},{24,28},{28,24},{1,5},{5... | collective-permute-start | bytes 1544 | tf_op jit(solution)/shard_map/cond/branch_1_fun/ppermute | solution.py:293
  34.9 2.0 %collective-permute-done.26 = f32[1,128]{1,0:T(1,128)S(1)} collective-permute-done((f32[1,128]{1,0:T(1,128)S(1)}, f32[1,128]{1,0:T(1,128)S(1)}, u32[]{:S(2)}, u32[]{:S(2)}) %collective-permute-start.26) | collective-permute-done | bytes 544 | tf_op jit(solution)/shard_map/cond/branch_1_fun/ppermute | solution.py:293
  37.0 1.6 %collective-permute-start.27 = (f32[1,128]{1,0:T(1,128)S(1)}, f32[1,128]{1,0:T(1,128)S(1)}, u32[]{:S(2)}, u32[]{:S(2)}) collective-permute-start(f32[1,128]{1,0:T(1,128)S(1)} %add.51), channel_id=1, source_target_pairs={{0,8},{4,12},{8,0},{12,4},{16,24},{20,28},{24,16},{28,20},{1,9},{5... | collective-permute-start | bytes 1544 | tf_op jit(solution)/shard_map/cond/branch_1_fun/ppermute | solution.py:293
  38.5 2.1 %collective-permute-done.27 = f32[1,128]{1,0:T(1,128)S(1)} collective-permute-done((f32[1,128]{1,0:T(1,128)S(1)}, f32[1,128]{1,0:T(1,128)S(1)}, u32[]{:S(2)}, u32[]{:S(2)}) %collective-permute-start.27) | collective-permute-done | bytes 544 | tf_op jit(solution)/shard_map/cond/branch_1_fun/ppermute | solution.py:293
  41.2 3.5 %collective-permute-start.32 = (f32[2,3,16,1024]{3,2,1,0:T(8,128)S(1)}, f32[2,3,16,1024]{3,2,1,0:T(8,128)S(1)}, u32[]{:S(2)}, u32[]{:S(2)}) collective-permute-start(f32[2,3,16,1024]{3,2,1,0:T(8,128)S(1)} %pick.21), channel_id=1, source_target_pairs={{0,16},{4,20},{8,24},{12,28},{16,0},{20,4},{24,8},{28,12},{1,17},{... | collective-permute-start | bytes 1179656 | tf_op jit(solution)/shard_map/cond/branch_1_fun/ppermute | solution.py:293
  45.4 2.5 %collective-permute-start.39 = (f32[3,16,1024]{2,1,0:T(8,128)S(1)}, f32[3,16,1024]{2,1,0:T(8,128)S(1)}, u32[]{:S(2)}, u32[]{:S(2)}) collective-permute-start(f32[3,16,1024]{2,1,0:T(8,128)S(1)} %get-tuple-element.149), channel_id=1, source_target_pairs={{0,4},{4,0},{8,12},{12,8},{16,20},{20,16},{24,28},{28,24},{1,5},{5... | collective-permute-start | bytes 589832 | tf_op jit(solution)/shard_map/cond/branch_1_fun/ppermute | solution.py:293
  48.0 15.3 %collective-permute-done.28 = f32[1,128]{1,0:T(1,128)S(1)} collective-permute-done((f32[1,128]{1,0:T(1,128)S(1)}, f32[1,128]{1,0:T(1,128)S(1)}, u32[]{:S(2)}, u32[]{:S(2)}) %collective-permute-start.28) | collective-permute-done | bytes 544 | tf_op jit(solution)/shard_map/cond/branch_1_fun/ppermute | solution.py:293
  63.3 2.6 %collective-permute-start.41 = (f32[3,16,1024]{2,1,0:T(8,128)S(1)}, f32[3,16,1024]{2,1,0:T(8,128)S(1)}, u32[]{:S(2)}, u32[]{:S(2)}) collective-permute-start(f32[3,16,1024]{2,1,0:T(8,128)S(1)} %get-tuple-element.151), channel_id=1, source_target_pairs={{0,12},{4,8},{8,4},{12,0},{16,28},{20,24},{24,20},{28,16},{1,13},{... | collective-permute-start | bytes 589832 | tf_op jit(solution)/shard_map/cond/branch_1_fun/ppermute | solution.py:293
  69.1 1.9 %collective-permute-start.37 = (f32[3,16,1024]{2,1,0:T(8,128)S(1)}, f32[3,16,1024]{2,1,0:T(8,128)S(1)}, u32[]{:S(2)}, u32[]{:S(2)}) collective-permute-start(f32[3,16,1024]{2,1,0:T(8,128)S(1)} %get-tuple-element.145), channel_id=1, source_target_pairs={{0,12},{4,8},{8,4},{12,0},{16,28},{20,24},{24,20},{28,16},{1,13},{... | collective-permute-start | bytes 589832 | tf_op jit(solution)/shard_map/cond/branch_1_fun/ppermute | solution.py:293
  72.5 3.1 %collective-permute-done.41.refs_3_ = f32[3,16,1024]{2,1,0:T(8,128)S(1)} collective-permute-done((f32[3,16,1024]{2,1,0:T(8,128)S(1)}, f32[3,16,1024]{2,1,0:T(8,128)S(1)}, u32[]{:S(2)}, u32[]{:S(2)}) %collective-permute-start.41) | collective-permute-done | bytes 196640 | tf_op jit(solution)/shard_map/cond/branch_1_fun/ppermute | solution.py:293
  77.6 1.5 %weigh.5 = f32[1]{0:T(128)} custom-call(s32[6]{0:T(128)S(1)} %get-tuple-element.114.at_ref.refs_0_, f32[1,128]{1,0:T(1,128)} %add.55.refs_1_), custom_call_target="tpu_custom_call" | custom-call | tf_op jit(solution)/shard_map/cond/branch_1_fun/weigh/pallas_call | solution.py:174
  79.5 4.4 %collective-permute-done.37.refs_3_ = f32[3,16,1024]{2,1,0:T(8,128)S(1)} collective-permute-done((f32[3,16,1024]{2,1,0:T(8,128)S(1)}, f32[3,16,1024]{2,1,0:T(8,128)S(1)}, u32[]{:S(2)}, u32[]{:S(2)}) %collective-permute-start.37) | collective-permute-done | bytes 196640 | tf_op jit(solution)/shard_map/cond/branch_1_fun/ppermute | solution.py:293
  84.0 1.5 %place.11 = f32[1,3,32,4096]{3,2,1,0:T(8,128)} custom-call(s32[6]{0:T(128)S(1)} %get-tuple-element.114.at_ref.refs_0_, f32[3,16,1024]{2,1,0:T(8,128)S(1)} %get-tuple-element.142.refs_0_, f32[3,16,1024]{2,1,0:T(8,128)S(1)} %collective-permute-done.35.refs_1_, f32[3,16,1024]{2,1,0:T(8,128)S(1)} %collective-permute-done.36.refs_2_, ...), custom_call_target="tpu_custom_call", output_to_operand_aliasing={{}: (5, {})} | custom-call | tf_op jit(solution)/shard_map/cond/branch_1_fun/place/pallas_call | solution.py:208
  (48 shorter events, 11.1 us)
Async XLA Ops:
  0.6 3.7 %copy-start.3 = (s32[256]{0:T(256)S(1)}, s32[256]{0:T(256)}, u32[]{:S(2)}) copy-start(s32[256]{0:T(256)} %param.12) | copy-start | bytes 3076
  0.6 3.7 %copy-start.4 = (f32[256]{0:T(256)S(1)}, f32[256]{0:T(256)}, u32[]{:S(2)}) copy-start(f32[256]{0:T(256)} %param.13) | copy-start | bytes 3076
  0.7 3.7 %copy-start.5 = (f32[256]{0:T(256)S(1)}, f32[256]{0:T(256)}, u32[]{:S(2)}) copy-start(f32[256]{0:T(256)} %param.14) | copy-start | bytes 3076
  4.4 11.6 %collective-permute-start.21 = (f32[4,8,4096]{2,1,0:T(8,128)}, f32[4,8,4096]{2,1,0:T(8,128)S(1)}, u32[]{:S(2)}, u32[]{:S(2)}) collective-permute-start(f32[4,8,4096]{2,1,0:T(8,128)} %get-tuple-element.121), channel_id=1, source_target_pairs={{0,1},{1,2},{2,3},{4,5},{5,6},{6,7},{8,9},{9,10},{10,11},{12,13},{... | collective-permute-start | bytes 1572872 | tf_op jit(solution)/shard_map/cond/branch_1_fun/ppermute | solution.py:345
  6.8 9.2 %collective-permute-start.22 = (f32[4,8,4096]{2,1,0:T(8,128)}, f32[4,8,4096]{2,1,0:T(8,128)S(1)}, u32[]{:S(2)}, u32[]{:S(2)}) collective-permute-start(f32[4,8,4096]{2,1,0:T(8,128)} %get-tuple-element.122), channel_id=1, source_target_pairs={{1,0},{2,1},{3,2},{5,4},{6,5},{7,6},{9,8},{10,9},{11,10},{13,12},{... | collective-permute-start | bytes 1572872 | tf_op jit(solution)/shard_map/cond/branch_1_fun/ppermute | solution.py:346
  12.0 13.2 %collective-permute-start.23 = (f32[3,16,1024]{2,1,0:T(8,128)S(1)}, f32[3,16,1024]{2,1,0:T(8,128)S(1)}, u32[]{:S(2)}, u32[]{:S(2)}) collective-permute-start(f32[3,16,1024]{2,1,0:T(8,128)S(1)} %get-tuple-element.126), channel_id=1, source_target_pairs={{0,4},{4,0},{8,12},{12,8},{16,20},{20,16},{24,28},{28,24},{1,5},{5... | collective-permute-start | bytes 589832 | tf_op jit(solution)/shard_map/cond/branch_1_fun/ppermute | solution.py:293
  14.4 10.8 %collective-permute-start.24 = (f32[3,16,1024]{2,1,0:T(8,128)S(1)}, f32[3,16,1024]{2,1,0:T(8,128)S(1)}, u32[]{:S(2)}, u32[]{:S(2)}) collective-permute-start(f32[3,16,1024]{2,1,0:T(8,128)S(1)} %get-tuple-element.127), channel_id=1, source_target_pairs={{0,8},{4,12},{8,0},{12,4},{16,24},{20,28},{24,16},{28,20},{1,9},{5... | collective-permute-start | bytes 589832 | tf_op jit(solution)/shard_map/cond/branch_1_fun/ppermute | solution.py:293
  16.0 9.2 %collective-permute-start.25 = (f32[3,16,1024]{2,1,0:T(8,128)S(1)}, f32[3,16,1024]{2,1,0:T(8,128)S(1)}, u32[]{:S(2)}, u32[]{:S(2)}) collective-permute-start(f32[3,16,1024]{2,1,0:T(8,128)S(1)} %get-tuple-element.128), channel_id=1, source_target_pairs={{0,12},{4,8},{8,4},{12,0},{16,28},{20,24},{24,20},{28,16},{1,13},{... | collective-permute-start | bytes 589832 | tf_op jit(solution)/shard_map/cond/branch_1_fun/ppermute | solution.py:293
  21.6 19.0 %collective-permute-start.29 = (f32[3,16,1024]{2,1,0:T(8,128)S(1)}, f32[3,16,1024]{2,1,0:T(8,128)S(1)}, u32[]{:S(2)}, u32[]{:S(2)}) collective-permute-start(f32[3,16,1024]{2,1,0:T(8,128)S(1)} %get-tuple-element.130), channel_id=1, source_target_pairs={{0,4},{4,0},{8,12},{12,8},{16,20},{20,16},{24,28},{28,24},{1,5},{5... | collective-permute-start | bytes 589832 | tf_op jit(solution)/shard_map/cond/branch_1_fun/ppermute | solution.py:293
  23.6 17.0 %collective-permute-start.30 = (f32[3,16,1024]{2,1,0:T(8,128)S(1)}, f32[3,16,1024]{2,1,0:T(8,128)S(1)}, u32[]{:S(2)}, u32[]{:S(2)}) collective-permute-start(f32[3,16,1024]{2,1,0:T(8,128)S(1)} %get-tuple-element.131), channel_id=1, source_target_pairs={{0,8},{4,12},{8,0},{12,4},{16,24},{20,28},{24,16},{28,20},{1,9},{5... | collective-permute-start | bytes 589832 | tf_op jit(solution)/shard_map/cond/branch_1_fun/ppermute | solution.py:293
  25.2 15.5 %collective-permute-start.31 = (f32[3,16,1024]{2,1,0:T(8,128)S(1)}, f32[3,16,1024]{2,1,0:T(8,128)S(1)}, u32[]{:S(2)}, u32[]{:S(2)}) collective-permute-start(f32[3,16,1024]{2,1,0:T(8,128)S(1)} %get-tuple-element.132), channel_id=1, source_target_pairs={{0,12},{4,8},{8,4},{12,0},{16,28},{20,24},{24,20},{28,16},{1,13},{... | collective-permute-start | bytes 589832 | tf_op jit(solution)/shard_map/cond/branch_1_fun/ppermute | solution.py:293
  25.8 18.9 %collective-permute-start.38 = (f32[2,3,16,1024]{3,2,1,0:T(8,128)S(1)}, f32[2,3,16,1024]{3,2,1,0:T(8,128)S(1)}, u32[]{:S(2)}, u32[]{:S(2)}) collective-permute-start(f32[2,3,16,1024]{3,2,1,0:T(8,128)S(1)} %pick.20), channel_id=1, source_target_pairs={{0,16},{4,20},{8,24},{12,28},{16,0},{20,4},{24,8},{28,12},{1,17},{... | collective-permute-start | bytes 1179656 | tf_op jit(solution)/shard_map/cond/branch_1_fun/ppermute | solution.py:293
  33.3 3.6 %collective-permute-start.26 = (f32[1,128]{1,0:T(1,128)S(1)}, f32[1,128]{1,0:T(1,128)S(1)}, u32[]{:S(2)}, u32[]{:S(2)}) collective-permute-start(f32[1,128]{1,0:T(1,128)S(1)} %misfit.5), channel_id=1, source_target_pairs={{0,4},{4,0},{8,12},{12,8},{16,20},{20,16},{24,28},{28,24},{1,5},{5... | collective-permute-start | bytes 1544 | tf_op jit(solution)/shard_map/cond/branch_1_fun/ppermute | solution.py:293
  37.0 3.6 %collective-permute-start.27 = (f32[1,128]{1,0:T(1,128)S(1)}, f32[1,128]{1,0:T(1,128)S(1)}, u32[]{:S(2)}, u32[]{:S(2)}) collective-permute-start(f32[1,128]{1,0:T(1,128)S(1)} %add.51), channel_id=1, source_target_pairs={{0,8},{4,12},{8,0},{12,4},{16,24},{20,28},{24,16},{28,20},{1,9},{5... | collective-permute-start | bytes 1544 | tf_op jit(solution)/shard_map/cond/branch_1_fun/ppermute | solution.py:293
  41.2 24.7 %collective-permute-start.32 = (f32[2,3,16,1024]{3,2,1,0:T(8,128)S(1)}, f32[2,3,16,1024]{3,2,1,0:T(8,128)S(1)}, u32[]{:S(2)}, u32[]{:S(2)}) collective-permute-start(f32[2,3,16,1024]{3,2,1,0:T(8,128)S(1)} %pick.21), channel_id=1, source_target_pairs={{0,16},{4,20},{8,24},{12,28},{16,0},{20,4},{24,8},{28,12},{1,17},{... | collective-permute-start | bytes 1179656 | tf_op jit(solution)/shard_map/cond/branch_1_fun/ppermute | solution.py:293
  45.4 22.3 %collective-permute-start.39 = (f32[3,16,1024]{2,1,0:T(8,128)S(1)}, f32[3,16,1024]{2,1,0:T(8,128)S(1)}, u32[]{:S(2)}, u32[]{:S(2)}) collective-permute-start(f32[3,16,1024]{2,1,0:T(8,128)S(1)} %get-tuple-element.149), channel_id=1, source_target_pairs={{0,4},{4,0},{8,12},{12,8},{16,20},{20,16},{24,28},{28,24},{1,5},{5... | collective-permute-start | bytes 589832 | tf_op jit(solution)/shard_map/cond/branch_1_fun/ppermute | solution.py:293
  48.0 15.3 %collective-permute-start.28 = (f32[1,128]{1,0:T(1,128)S(1)}, f32[1,128]{1,0:T(1,128)S(1)}, u32[]{:S(2)}, u32[]{:S(2)}) collective-permute-start(f32[1,128]{1,0:T(1,128)S(1)} %add.52), channel_id=1, source_target_pairs={{0,16},{4,20},{8,24},{12,28},{16,0},{20,4},{24,8},{28,12},{1,17},{... | collective-permute-start | bytes 1544 | tf_op jit(solution)/shard_map/cond/branch_1_fun/ppermute | solution.py:293
  63.3 7.8 %collective-permute-start.40 = (f32[3,16,1024]{2,1,0:T(8,128)S(1)}, f32[3,16,1024]{2,1,0:T(8,128)S(1)}, u32[]{:S(2)}, u32[]{:S(2)}) collective-permute-start(f32[3,16,1024]{2,1,0:T(8,128)S(1)} %get-tuple-element.150), channel_id=1, source_target_pairs={{0,8},{4,12},{8,0},{12,4},{16,24},{20,28},{24,16},{28,20},{1,9},{5... | collective-permute-start | bytes 589832 | tf_op jit(solution)/shard_map/cond/branch_1_fun/ppermute | solution.py:293
  63.3 12.3 %collective-permute-start.41 = (f32[3,16,1024]{2,1,0:T(8,128)S(1)}, f32[3,16,1024]{2,1,0:T(8,128)S(1)}, u32[]{:S(2)}, u32[]{:S(2)}) collective-permute-start(f32[3,16,1024]{2,1,0:T(8,128)S(1)} %get-tuple-element.151), channel_id=1, source_target_pairs={{0,12},{4,8},{8,4},{12,0},{16,28},{20,24},{24,20},{28,16},{1,13},{... | collective-permute-start | bytes 589832 | tf_op jit(solution)/shard_map/cond/branch_1_fun/ppermute | solution.py:293
  66.6 2.5 %collective-permute-start.33 = (f32[1,128]{1,0:T(1,128)S(1)}, f32[1,128]{1,0:T(1,128)S(1)}, u32[]{:S(2)}, u32[]{:S(2)}) collective-permute-start(f32[1,128]{1,0:T(1,128)S(1)} %add.53), channel_id=1, source_target_pairs={{0,1},{1,0},{2,3},{3,2},{4,5},{5,4},{6,7},{7,6},{8,9},{9,8},{10,11... | collective-permute-start | bytes 1544 | tf_op jit(solution)/shard_map/cond/branch_1_fun/ppermute | solution.py:159
  67.6 11.6 %collective-permute-start.35 = (f32[3,16,1024]{2,1,0:T(8,128)S(1)}, f32[3,16,1024]{2,1,0:T(8,128)S(1)}, u32[]{:S(2)}, u32[]{:S(2)}) collective-permute-start(f32[3,16,1024]{2,1,0:T(8,128)S(1)} %get-tuple-element.143), channel_id=1, source_target_pairs={{0,4},{4,0},{8,12},{12,8},{16,20},{20,16},{24,28},{28,24},{1,5},{5... | collective-permute-start | bytes 589832 | tf_op jit(solution)/shard_map/cond/branch_1_fun/ppermute | solution.py:293
  67.7 11.8 %collective-permute-start.36 = (f32[3,16,1024]{2,1,0:T(8,128)S(1)}, f32[3,16,1024]{2,1,0:T(8,128)S(1)}, u32[]{:S(2)}, u32[]{:S(2)}) collective-permute-start(f32[3,16,1024]{2,1,0:T(8,128)S(1)} %get-tuple-element.144), channel_id=1, source_target_pairs={{0,8},{4,12},{8,0},{12,4},{16,24},{20,28},{24,16},{28,20},{1,9},{5... | collective-permute-start | bytes 589832 | tf_op jit(solution)/shard_map/cond/branch_1_fun/ppermute | solution.py:293
  69.1 14.8 %collective-permute-start.37 = (f32[3,16,1024]{2,1,0:T(8,128)S(1)}, f32[3,16,1024]{2,1,0:T(8,128)S(1)}, u32[]{:S(2)}, u32[]{:S(2)}) collective-permute-start(f32[3,16,1024]{2,1,0:T(8,128)S(1)} %get-tuple-element.145), channel_id=1, source_target_pairs={{0,12},{4,8},{8,4},{12,0},{16,28},{20,24},{24,20},{28,16},{1,13},{... | collective-permute-start | bytes 589832 | tf_op jit(solution)/shard_map/cond/branch_1_fun/ppermute | solution.py:293
  71.1 6.0 %collective-permute-start.34 = (f32[1,128]{1,0:T(1,128)S(1)}, f32[1,128]{1,0:T(1,128)S(1)}, u32[]{:S(2)}, u32[]{:S(2)}) collective-permute-start(f32[1,128]{1,0:T(1,128)S(1)} %add.54), channel_id=1, source_target_pairs={{0,2},{1,3},{2,0},{3,1},{4,6},{5,7},{6,4},{7,5},{8,10},{9,11},{10,... | collective-permute-start | bytes 1544 | tf_op jit(solution)/shard_map/cond/branch_1_fun/ppermute | solution.py:159
  (3 other events, 6.5 us)
